TPU v7x, 32 devices: a whole 2x2x4 slice. The times are simulated.
32 devices in a mesh: dp: 8 (over z, x), tm: 4 (over y, core).
Axes of the slice: x: 2, y: 2, z: 4, core: 2. Of those that a mesh axis runs over, the one named last changes fastest.
Arguments:
- clips: bfloat16 [8, 32, 16, 16, 256], P('dp', 'tm'), may hold values from -6 to 6
- frame_counts: int32 [8], P('dp'), may hold values from 5 to 32, as said below
- weight: bfloat16 [6912, 256], P('dp'), may hold values from -0.078125 to 0.078125
- gain: float32 [256], replicated, may hold values from 0.1 to 1.9
- bias: float32 [256], replicated, may hold values from -3 to 3
- cotangent: bfloat16 [8, 16, 8, 8, 256], P('dp', 'tm'), may hold values from -6 to 6
Outputs:
- output: bfloat16 [8, 16, 8, 8, 256], P('dp', 'tm')
- input_grad: bfloat16 [8, 32, 16, 16, 256], P('dp', 'tm')
- weight_grad: float32 [6912, 256], P('dp')
Inputs may be any that keep to these rules, and one draw needn't show every extreme that they name: frame_counts[c] frames of clip c are valid, the remaining slots are padding; in every draw some clip uses all 32 slots.
All inputs are finite; a program needn't handle non-finite values.
Results may differ from a plain program's by a relative error of at most 0.0048.
Values may be sent and summed in bfloat16 or wider, within the bound.
A program may use at most 64 MiB of HBM per device.

v0:
```python
import jax
import jax.numpy as jnp
from jax import lax
from jax.sharding import PartitionSpec as P

GROUPS = 32
EPS = 1e-06


def shifted(value, axis, by):
    devices = lax.axis_size(axis)
    pairs = [(i, i + by) for i in range(devices) if 0 <= i + by < devices]
    return lax.ppermute(value, axis, pairs)


def unfold(padded, frames_out, rows_out, cols_out):
    tap_list = []
    for step_t in range(3):
        for step_r in range(3):
            for step_c in range(3):
                tap_piece = padded[
                    step_t : step_t + 2 * frames_out : 2,
                    step_r : step_r + 2 * rows_out : 2,
                    step_c : step_c + 2 * cols_out : 2,
                    :,
                ]
                tap_list.append(tap_piece.reshape(frames_out * rows_out * cols_out, -1))
    return jnp.concatenate(tap_list, axis=1)


def spread_taps(values, data_axis, tap_axis, length):
    moved = jnp.moveaxis(values, tap_axis, 0)
    count = moved.shape[data_axis + 1]
    width_list = [(0, 0)] * (moved.ndim - 1)
    after = list(width_list)
    after[data_axis] = (0, 1)
    before = list(width_list)
    before[data_axis] = (1, 0)
    even_part = jnp.pad(moved[0], after) + jnp.pad(moved[2], before)
    odd_part = jnp.pad(moved[1], after)
    joined = jnp.stack([even_part, odd_part], axis=data_axis + 1)
    shape_new = list(even_part.shape)
    shape_new[data_axis] = 2 * (count + 1)
    joined = joined.reshape(shape_new)
    return lax.slice_in_dim(joined, 0, length, axis=data_axis)


def fold_back(columns, padded_shape, frames_out, rows_out, cols_out):
    channels = padded_shape[3]
    blocks = columns.reshape(frames_out, rows_out, cols_out, 3, 3, 3, channels)
    blocks = spread_taps(blocks, 0, 3, padded_shape[0])
    blocks = spread_taps(blocks, 1, 3, padded_shape[1])
    blocks = spread_taps(blocks, 2, 3, padded_shape[2])
    return blocks


def silu_slope(preact):
    sig = jax.nn.sigmoid(preact)
    return sig * (1.0 + preact * (1.0 - sig))


def shards(clips, frame_counts, weight, gain, bias, cotangent):
    clip_data = clips[0]
    cot_block = cotangent[0]
    frame_count, row_count, col_count, channels = clip_data.shape
    width_g = channels // GROUPS
    first_frame = lax.axis_index("tm") * frame_count
    frame_mask = (first_frame + jnp.arange(frame_count) < frame_counts[0]).astype(jnp.float32)[
        :, None, None, None
    ]
    mask_group = frame_mask[..., None]
    entries = frame_counts[0].astype(jnp.float32) * (row_count * col_count * width_g)
    values = clip_data.astype(jnp.float32).reshape(
        frame_count, row_count, col_count, GROUPS, width_g
    )
    sum_first, sum_second = lax.psum(
        (
            jnp.sum(values * mask_group, axis=(0, 1, 2, 4)),
            jnp.sum(values * values * mask_group, axis=(0, 1, 2, 4)),
        ),
        "tm",
    )
    group_mean = sum_first / entries
    variance = sum_second / entries - group_mean * group_mean
    inv_std = lax.rsqrt(variance + EPS)
    normed_g = (values - group_mean[:, None]) * inv_std[:, None]
    normed = normed_g.reshape(frame_count, row_count, col_count, channels)
    preact = normed * gain + bias
    hidden = (jax.nn.silu(preact) * frame_mask).astype(jnp.bfloat16)
    earlier = shifted(hidden[-2:], "tm", 1)
    padded = jnp.pad(jnp.concatenate([earlier, hidden], axis=0), ((0, 0), (1, 0), (1, 0), (0, 0)))
    frames_out, rows_out, cols_out = (frame_count // 2, row_count // 2, col_count // 2)
    patches = unfold(padded, frames_out, rows_out, cols_out)
    cot_rows = cot_block.reshape(-1, channels)
    full_weight = lax.all_gather(weight, "dp", axis=0, tiled=True)
    out_rows = jnp.dot(patches, full_weight, preferred_element_type=jnp.float32)
    out_block = out_rows.astype(jnp.bfloat16).reshape(frames_out, rows_out, cols_out, channels)
    dcols = lax.dot_general(
        cot_rows, full_weight, (((1,), (1,)), ((), ())), preferred_element_type=jnp.float32
    )
    dpad = fold_back(dcols, padded.shape, frames_out, rows_out, cols_out)
    passed = shifted(dpad[:2, 1:, 1:, :], "tm", -1)
    dlocal = dpad[2:, 1:, 1:, :]
    dhidden = jnp.concatenate([dlocal[:-2], dlocal[-2:] + passed], axis=0)
    dnormed = dhidden * frame_mask * silu_slope(preact) * gain
    grad_norm = dnormed.reshape(frame_count, row_count, col_count, GROUPS, width_g)
    back_first, back_second = lax.psum(
        (jnp.sum(grad_norm, axis=(0, 1, 2, 4)), jnp.sum(grad_norm * normed_g, axis=(0, 1, 2, 4))),
        "tm",
    )
    input_grad = (
        mask_group
        * inv_std[:, None]
        * (grad_norm - back_first[:, None] / entries - normed_g * back_second[:, None] / entries)
    )
    input_grad = input_grad.reshape(frame_count, row_count, col_count, channels).astype(
        jnp.bfloat16
    )
    local_grad = lax.dot_general(
        patches, cot_rows, (((0,), (0,)), ((), ())), preferred_element_type=jnp.float32
    )
    clip_grad = lax.psum(local_grad, "tm")
    weight_grad = lax.psum_scatter(clip_grad, "dp", scatter_dimension=0, tiled=True)
    return (out_block[None], input_grad[None], weight_grad)


def solution(mesh):
    placed = (
        P("dp", "tm", None, None, None),
        P("dp"),
        P("dp", None),
        P(),
        P(),
        P("dp", "tm", None, None, None),
    )
    return jax.shard_map(
        shards,
        mesh=mesh,
        in_specs=placed,
        out_specs=(P("dp", "tm", None, None, None), P("dp", "tm", None, None, None), P("dp", None)),
        check_vma=False,
    )
```

profile of v0, /device:TPU:0, one launch (start us, length us, event | category | flops | bytes accessed | tf_op | source)
XLA Modules:
  0.0 398.6 jit_solution(1808083092063788715)
XLA Ops:
  8.6 1.8 fusion.18
  10.9 8.4 %all-reduce.11 = (f32[32]{0:T(128)S(1)}, f32[32]{0:T(128)S(1)}) all-reduce(f32[32]{0:T(128)S(1)} %reduce_sum.51, f32[32]{0:T(128)S(1)} %reduce_sum.54), channel_id=1, replica_groups=mesh['dp'=8,'tm'=4] {'tm'}, use_global_device_ids=true, to_apply=%region_2.0 | all-reduce | flops 64 | bytes 512 | tf_op jit(solution)/shard_map/psum | solution.py:76
  19.6 2.1 fusion.15
  21.7 1.3 collective-permute-start
  23.0 1.1 collective-permute-done
  24.2 1.0 fusion.38
  25.2 1.2 slice.155
  26.4 1.2 slice.154
  32.6 1.5 slice.147
  34.1 9.8 %slice.146 = bf16[4,8,8,256]{3,2,1,0:T(8,128)(2,1)} slice(bf16[10,17,17,256]{3,2,1,0:T(8,128)(2,1)S(1)} %fusion.38), slice={[1:9:2], [2:17:2], [1:17:2], [0:256:1]} | slice | bytes 262144 | tf_op jit(solution)/shard_map/slice | solution.py:21
  43.9 9.7 %slice.145 = bf16[4,8,8,256]{3,2,1,0:T(8,128)(2,1)} slice(bf16[10,17,17,256]{3,2,1,0:T(8,128)(2,1)S(1)} %fusion.38), slice={[1:9:2], [2:17:2], [0:16:2], [0:256:1]} | slice | bytes 262144 | tf_op jit(solution)/shard_map/slice | solution.py:21
  53.6 9.8 %slice.144 = bf16[4,8,8,256]{3,2,1,0:T(8,128)(2,1)} slice(bf16[10,17,17,256]{3,2,1,0:T(8,128)(2,1)S(1)} %fusion.38), slice={[1:9:2], [1:17:2], [2:17:2], [0:256:1]} | slice | bytes 262144 | tf_op jit(solution)/shard_map/slice | solution.py:21
  63.4 9.7 %slice.143 = bf16[4,8,8,256]{3,2,1,0:T(8,128)(2,1)} slice(bf16[10,17,17,256]{3,2,1,0:T(8,128)(2,1)S(1)} %fusion.38), slice={[1:9:2], [1:17:2], [1:17:2], [0:256:1]} | slice | bytes 262144 | tf_op jit(solution)/shard_map/slice | solution.py:21
  73.1 9.7 %slice.142 = bf16[4,8,8,256]{3,2,1,0:T(8,128)(2,1)} slice(bf16[10,17,17,256]{3,2,1,0:T(8,128)(2,1)S(1)} %fusion.38), slice={[1:9:2], [1:17:2], [0:16:2], [0:256:1]} | slice | bytes 262144 | tf_op jit(solution)/shard_map/slice | solution.py:21
  82.8 9.7 %slice.141 = bf16[4,8,8,256]{3,2,1,0:T(8,128)(2,1)} slice(bf16[10,17,17,256]{3,2,1,0:T(8,128)(2,1)S(1)} %fusion.38), slice={[1:9:2], [0:16:2], [2:17:2], [0:256:1]} | slice | bytes 262144 | tf_op jit(solution)/shard_map/slice | solution.py:21
  92.5 9.7 %slice.140 = bf16[4,8,8,256]{3,2,1,0:T(8,128)(2,1)} slice(bf16[10,17,17,256]{3,2,1,0:T(8,128)(2,1)S(1)} %fusion.38), slice={[1:9:2], [0:16:2], [1:17:2], [0:256:1]} | slice | bytes 262144 | tf_op jit(solution)/shard_map/slice | solution.py:21
  102.2 9.7 %slice.139 = bf16[4,8,8,256]{3,2,1,0:T(8,128)(2,1)} slice(bf16[10,17,17,256]{3,2,1,0:T(8,128)(2,1)S(1)} %fusion.38), slice={[1:9:2], [0:16:2], [0:16:2], [0:256:1]} | slice | bytes 262144 | tf_op jit(solution)/shard_map/slice | solution.py:21
  111.9 9.8 %slice.138 = bf16[4,8,8,256]{3,2,1,0:T(8,128)(2,1)} slice(bf16[10,17,17,256]{3,2,1,0:T(8,128)(2,1)S(1)} %fusion.38), slice={[0:8:2], [2:17:2], [2:17:2], [0:256:1]} | slice | bytes 262144 | tf_op jit(solution)/shard_map/slice | solution.py:21
  121.7 9.7 %slice.137 = bf16[4,8,8,256]{3,2,1,0:T(8,128)(2,1)} slice(bf16[10,17,17,256]{3,2,1,0:T(8,128)(2,1)S(1)} %fusion.38), slice={[0:8:2], [2:17:2], [1:17:2], [0:256:1]} | slice | bytes 262144 | tf_op jit(solution)/shard_map/slice | solution.py:21
  131.4 9.7 %slice.136 = bf16[4,8,8,256]{3,2,1,0:T(8,128)(2,1)} slice(bf16[10,17,17,256]{3,2,1,0:T(8,128)(2,1)S(1)} %fusion.38), slice={[0:8:2], [2:17:2], [0:16:2], [0:256:1]} | slice | bytes 262144 | tf_op jit(solution)/shard_map/slice | solution.py:21
  141.1 9.8 %slice.135 = bf16[4,8,8,256]{3,2,1,0:T(8,128)(2,1)} slice(bf16[10,17,17,256]{3,2,1,0:T(8,128)(2,1)S(1)} %fusion.38), slice={[0:8:2], [1:17:2], [2:17:2], [0:256:1]} | slice | bytes 262144 | tf_op jit(solution)/shard_map/slice | solution.py:21
  150.9 9.7 %slice.134 = bf16[4,8,8,256]{3,2,1,0:T(8,128)(2,1)} slice(bf16[10,17,17,256]{3,2,1,0:T(8,128)(2,1)S(1)} %fusion.38), slice={[0:8:2], [1:17:2], [1:17:2], [0:256:1]} | slice | bytes 262144 | tf_op jit(solution)/shard_map/slice | solution.py:21
  160.6 9.7 %slice.133 = bf16[4,8,8,256]{3,2,1,0:T(8,128)(2,1)} slice(bf16[10,17,17,256]{3,2,1,0:T(8,128)(2,1)S(1)} %fusion.38), slice={[0:8:2], [1:17:2], [0:16:2], [0:256:1]} | slice | bytes 262144 | tf_op jit(solution)/shard_map/slice | solution.py:21
  170.3 9.8 %slice.132 = bf16[4,8,8,256]{3,2,1,0:T(8,128)(2,1)} slice(bf16[10,17,17,256]{3,2,1,0:T(8,128)(2,1)S(1)} %fusion.38), slice={[0:8:2], [0:16:2], [2:17:2], [0:256:1]} | slice | bytes 262144 | tf_op jit(solution)/shard_map/slice | solution.py:21
  180.1 9.7 %slice.131 = bf16[4,8,8,256]{3,2,1,0:T(8,128)(2,1)} slice(bf16[10,17,17,256]{3,2,1,0:T(8,128)(2,1)S(1)} %fusion.38), slice={[0:8:2], [0:16:2], [1:17:2], [0:256:1]} | slice | bytes 262144 | tf_op jit(solution)/shard_map/slice | solution.py:21
  189.8 9.7 %slice.130 = bf16[4,8,8,256]{3,2,1,0:T(8,128)(2,1)} slice(bf16[10,17,17,256]{3,2,1,0:T(8,128)(2,1)S(1)} %fusion.38), slice={[0:8:2], [0:16:2], [0:16:2], [0:256:1]} | slice | bytes 262144 | tf_op jit(solution)/shard_map/slice | solution.py:21
  199.6 1.5 slice.156
  201.1 1.0 constant_dynamic-update-slice_fusion.26
  202.1 0.9 constant_dynamic-update-slice_fusion.25
  203.0 0.9 constant_dynamic-update-slice_fusion.24
  203.9 0.9 constant_dynamic-update-slice_fusion.23
  204.8 0.9 constant_dynamic-update-slice_fusion.22
  212.5 1.7 copy-done.3
  214.3 4.1 %fusion.43 = f32[6912,256]{1,0:T(8,128)} fusion(bf16[256,6912]{1,0:T(8,128)(2,1)S(1)} %constant_dynamic-update-slice_fusion, bf16[256,256]{1,0:T(8,128)(2,1)S(1)} %bitcast.127), kind=kOutput, calls=%fused_computation.105 | convolution fusion | flops 905969664 | bytes 10747904 | tf_op jit(solution)/shard_map/dot_general | solution.py:119
  218.9 3.1 convolution_bitcast_fusion
  228.8 3.1 copy.39
  231.9 3.5 reshape.271
  235.4 1.3 slice.183
  236.7 1.5 collective-permute-start.1
  238.2 1.9 slice_bitcast_fusion.7
  240.2 3.9 convolution_convert_fusion
  244.0 1.2 fusion.39
  245.3 1.3 fusion.41
  247.1 13.6 %all-reduce.10 = (f32[32]{0:T(128)S(1)}, f32[32]{0:T(128)S(1)}) all-reduce(f32[32]{0:T(128)S(1)} %reduce_sum.75, f32[32]{0:T(128)S(1)} %reduce_sum.72), channel_id=1, replica_groups=mesh['dp'=8,'tm'=4] {'tm'}, use_global_device_ids=true, to_apply=%region_11.12 | all-reduce | flops 64 | bytes 512 | tf_op jit(solution)/shard_map/psum | solution.py:107
  261.0 92.3 %reduce-scatter.2.cloned.1.call-done = f32[864,256]{1,0:T(8,128)} async-done(((f32[6912,256]{1,0:T(8,128)}), f32[864,256]{1,0:T(8,128)}) %reduce-scatter.2.cloned.1.call-update) | async-done | bytes 884752 | tf_op jit(solution)/shard_map/reduce_scatter | solution.py:123
  353.3 1.6 fusion.37
  354.9 35.1 %all-reduce.14.cloned.1.call-done = f32[864,256]{1,0:T(8,128)} async-done(((f32[864,256]{1,0:T(8,128)}), f32[864,256]{1,0:T(8,128)}) %all-reduce.14.cloned.1.call-update) | async-done | bytes 884752 | tf_op jit(solution)/shard_map/psum | solution.py:122
  390.0 2.1 copy.76
  (96 shorter events, 21.0 us)
Async XLA Ops:
  7.2 205.4 %copy-start = (bf16[1,4,8,8,256]{4,3,2,1,0:T(8,128)(2,1)S(1)}, bf16[1,4,8,8,256]{4,3,2,1,0:T(8,128)(2,1)}, u32[]{:S(2)}) copy-start(bf16[1,4,8,8,256]{4,3,2,1,0:T(8,128)(2,1)} %param.11) | copy-start | bytes 393220
  7.2 211.7 %all-gather.2.cloned.1.call-start = ((), (), s32[]{:S(2)}) async-start(), calls=%async_computation.1 | async-start | bytes 3981312 | tf_op jit(solution)/shard_map/all_gather | solution.py:95
  7.9 345.4 %reduce-scatter.2.cloned.1.call-start = ((), (), s32[]{:S(2)}) async-start(), calls=%async_computation.2 | async-start | bytes 7962624 | tf_op jit(solution)/shard_map/reduce_scatter | solution.py:123
  21.7 2.4 collective-permute-start
  201.1 11.1 %copy-start.9 = (bf16[4,8,8,256]{3,2,1,0:T(8,128)(2,1)S(1)}, bf16[4,8,8,256]{3,2,1,0:T(8,128)(2,1)}, u32[]{:S(2)}) copy-start(bf16[4,8,8,256]{3,2,1,0:T(8,128)(2,1)} %slice.142) | copy-start | bytes 393220
  201.1 11.2 %copy-start.8 = (bf16[4,8,8,256]{3,2,1,0:T(8,128)(2,1)S(1)}, bf16[4,8,8,256]{3,2,1,0:T(8,128)(2,1)}, u32[]{:S(2)}) copy-start(bf16[4,8,8,256]{3,2,1,0:T(8,128)(2,1)} %slice.143) | copy-start | bytes 393220
  201.1 11.2 %copy-start.7 = (bf16[4,8,8,256]{3,2,1,0:T(8,128)(2,1)S(1)}, bf16[4,8,8,256]{3,2,1,0:T(8,128)(2,1)}, u32[]{:S(2)}) copy-start(bf16[4,8,8,256]{3,2,1,0:T(8,128)(2,1)} %slice.144) | copy-start | bytes 393220
  201.1 11.2 %copy-start.6 = (bf16[4,8,8,256]{3,2,1,0:T(8,128)(2,1)S(1)}, bf16[4,8,8,256]{3,2,1,0:T(8,128)(2,1)}, u32[]{:S(2)}) copy-start(bf16[4,8,8,256]{3,2,1,0:T(8,128)(2,1)} %slice.145) | copy-start | bytes 393220
  201.1 11.2 %copy-start.5 = (bf16[4,8,8,256]{3,2,1,0:T(8,128)(2,1)S(1)}, bf16[4,8,8,256]{3,2,1,0:T(8,128)(2,1)}, u32[]{:S(2)}) copy-start(bf16[4,8,8,256]{3,2,1,0:T(8,128)(2,1)} %slice.146) | copy-start | bytes 393220
  212.5 1.8 copy-start.3
  218.4 171.6 %all-reduce.14.cloned.1.call-start = ((), (), s32[]{:S(2)}) async-start(), calls=%async_computation.3 | async-start | bytes 1769472 | tf_op jit(solution)/shard_map/psum | solution.py:122
  235.4 4.8 %copy-start.4 = (bf16[256,6912]{1,0:T(8,128)(2,1)S(1)}, bf16[256,6912]{1,0:T(8,128)(2,1)}, u32[]{:S(2)}) copy-start(bf16[256,6912]{1,0:T(8,128)(2,1)} %copy-done.3) | copy-start | bytes 10616836
  236.7 7.3 %collective-permute-start.1 = (f32[2,16,16,256]{3,2,1,0:T(8,128)S(1)}, f32[2,16,16,256]{3,2,1,0:T(8,128)S(1)}, u32[]{:S(2)}, u32[]{:S(2)}) collective-permute-start(f32[2,16,16,256]{3,2,1,0:T(8,128)S(1)} %slice.183), channel_id=1, source_target_pairs={{1,0},{2,1},{3,2},{5,4},{6,5},{7,6},{9,8},{10,9},{11,10},{13,12},{... | collective-permute-start | bytes 1572872 | tf_op jit(solution)/shard_map/ppermute | solution.py:13
  240.2 5.1 %copy-start.2 = (bf16[1,8,16,16,256]{4,3,2,1,0:T(8,128)(2,1)S(1)}, bf16[1,8,16,16,256]{4,3,2,1,0:T(8,128)(2,1)}, u32[]{:S(2)}) copy-start(bf16[1,8,16,16,256]{4,3,2,1,0:T(8,128)(2,1)} %param.6) | copy-start | bytes 3145732
  240.2 5.1 %copy-start.10 = (f32[256]{0:T(256)S(1)}, f32[256]{0:T(256)}, u32[]{:S(2)}) copy-start(f32[256]{0:T(256)} %param.10) | copy-start | bytes 3076
  240.2 5.1 %copy-start.11 = (f32[256]{0:T(256)S(1)}, f32[256]{0:T(256)}, u32[]{:S(2)}) copy-start(f32[256]{0:T(256)} %param.9) | copy-start | bytes 3076
  353.3 38.8 %copy-start.1 = (bf16[1,4,8,8,256]{4,3,2,1,0:T(8,128)(2,1)S(1)}, bf16[1,4,8,8,256]{4,3,2,1,0:T(8,128)(2,1)}, u32[]{:S(2)}) copy-start(bf16[1,4,8,8,256]{4,3,2,1,0:T(8,128)(2,1)} %param.11) | copy-start | bytes 393220
Sparse Core Ops, SparseCore 0:
  10.2 67.8 all-gather.1
  218.5 134.7 reduce-scatter.1
  355.8 34.1 all-reduce.13
where the time goes:
time: 399 us
  local copies, waits for them, and re-layouts  206 us (52%)
  waiting for transfers between devices  129 us (32%)
  blocking collectives  21.9 us (5%)
  between operations  15.1 us (4%)
  other arithmetic  12.5 us (3%)
  matrix products  11 us (3%)
    slice x27, local copies, waits for them, and re-layouts, unfold(): padded[step_t:step_t + 2 * frames_out:2, step_r:step_r + 2 * rows_out:2,...  176 us
    reduce_scatter x1, waiting for transfers between devices, shards(): lax.psum_scatter(clip_grad, 'dp', scatter_dimension=0, tiled=True)  92.3 us
    psum x1, waiting for transfers between devices, shards(): clip_grad = lax.psum(local_grad, 'tm')  35.1 us
    unnamed x51, local copies, waits for them, and re-layouts  15.1 us
    psum x1, blocking collectives, shards(): lax.psum((jnp.sum(grad_norm, axis=(0, 1, 2, 4)), jnp.sum(grad_norm * norm...  13.6 us
    psum x1, blocking collectives, shards(): lax.psum((jnp.sum(values * mask_group, axis=(0, 1, 2, 4)), jnp.sum(values...  8.37 us
  transfers between devices with their start and end apart: 5, of which 3 were waited for; matrix products, arithmetic and copies ran while one was open for 57% of the time, Pallas kernels for 0%

commit v1 on v0

--- a/solution.py
+++ b/solution.py
@@ -5,6 +5,12 @@
 
 GROUPS = 32
 EPS = 1e-06
+
+
+def gather_and_add(block, axis):
+    parts = lax.all_gather(block, axis, axis=0, tiled=False)
+    summed = parts.sum(axis=0)
+    return summed
 
 
 def shifted(value, axis, by):
@@ -119,7 +125,7 @@
     local_grad = lax.dot_general(
         patches, cot_rows, (((0,), (0,)), ((), ())), preferred_element_type=jnp.float32
     )
-    clip_grad = lax.psum(local_grad, "tm")
+    clip_grad = gather_and_add(local_grad, "tm")
     weight_grad = lax.psum_scatter(clip_grad, "dp", scatter_dimension=0, tiled=True)
     return (out_block[None], input_grad[None], weight_grad)
 

time: 399 us -> 603 us (1.51)
  waiting for transfers between devices: 129 us -> 323 us
  other arithmetic: 12.5 us -> 27.5 us
    all_gather x0 -> x1, waiting for transfers between devices: none -> 177 us  [gather_and_add(): parts = lax.all_gather(block, axis, axis=0, tiled=False)]
    all_gather x1, waiting for transfers between devices: 0.02 us -> 52.1 us  [shards(): full_weight = lax.all_gather(weight, 'dp', axis=0, tiled=True)]
    psum x1 -> x0, waiting for transfers between devices: 35.1 us -> none  [shards(): clip_grad = lax.psum(local_grad, 'tm')]
    reduce_sum x0 -> x1, other arithmetic: none -> 15 us  [gather_and_add(): summed = parts.sum(axis=0)]
    unnamed x51 -> x46, local copies, waits for them, and re-layouts: 15.1 us -> 14.8 us
  transfers between devices with their start and end apart: 5 -> 5, of which waited for: 3 -> 4; matrix products, arithmetic and copies ran while one was open for 57% -> 7% of each run, Pallas kernels for 0% -> 0%
where the time goes in v1:
time: 603 us
  waiting for transfers between devices  323 us (54%)
  local copies, waits for them, and re-layouts  205 us (34%)
  other arithmetic  27.5 us (5%)
  blocking collectives  17.8 us (3%)
  between operations  15 us (2%)
  matrix products  11 us (2%)
    all_gather x1, waiting for transfers between devices, gather_and_add(): parts = lax.all_gather(block, axis, axis=0, tiled=False)  177 us
    slice x27, local copies, waits for them, and re-layouts, unfold(): padded[step_t:step_t + 2 * frames_out:2, step_r:step_r + 2 * rows_out:2,...  176 us
    reduce_scatter x1, waiting for transfers between devices, shards(): lax.psum_scatter(clip_grad, 'dp', scatter_dimension=0, tiled=True)  92.2 us
    all_gather x1, waiting for transfers between devices, shards(): full_weight = lax.all_gather(weight, 'dp', axis=0, tiled=True)  52.1 us
    reduce_sum x1, other arithmetic, gather_and_add(): summed = parts.sum(axis=0)  15 us
    unnamed x46, local copies, waits for them, and re-layouts  14.8 us
  transfers between devices with their start and end apart: 5, of which 4 were waited for; matrix products, arithmetic and copies ran while one was open for 7% of the time, Pallas kernels for 0%

profile of v1, /device:TPU:0, one launch (start us, length us, event | category | flops | bytes accessed | tf_op | source)
XLA Modules:
  0.0 602.8 jit_solution(7198181999939417145)
XLA Ops:
  7.9 1.8 fusion.18
  10.2 8.4 %all-reduce.11 = (f32[32]{0:T(128)S(1)}, f32[32]{0:T(128)S(1)}) all-reduce(f32[32]{0:T(128)S(1)} %reduce_sum.59, f32[32]{0:T(128)S(1)} %reduce_sum.62), channel_id=1, replica_groups=mesh['dp'=8,'tm'=4] {'tm'}, use_global_device_ids=true, to_apply=%region_2.0 | all-reduce | flops 64 | bytes 512 | tf_op jit(solution)/shard_map/psum | solution.py:82
  18.9 2.0 fusion.15
  21.0 1.3 collective-permute-start
  22.3 1.1 collective-permute-done
  23.4 1.0 fusion.38
  24.4 9.8 %slice.130 = bf16[4,8,8,256]{3,2,1,0:T(8,128)(2,1)} slice(bf16[10,17,17,256]{3,2,1,0:T(8,128)(2,1)S(1)} %fusion.38), slice={[0:8:2], [0:16:2], [0:16:2], [0:256:1]} | slice | bytes 262144 | tf_op jit(solution)/shard_map/slice | solution.py:27
  34.2 9.7 %slice.131 = bf16[4,8,8,256]{3,2,1,0:T(8,128)(2,1)} slice(bf16[10,17,17,256]{3,2,1,0:T(8,128)(2,1)S(1)} %fusion.38), slice={[0:8:2], [0:16:2], [1:17:2], [0:256:1]} | slice | bytes 262144 | tf_op jit(solution)/shard_map/slice | solution.py:27
  44.0 9.8 %slice.132 = bf16[4,8,8,256]{3,2,1,0:T(8,128)(2,1)} slice(bf16[10,17,17,256]{3,2,1,0:T(8,128)(2,1)S(1)} %fusion.38), slice={[0:8:2], [0:16:2], [2:17:2], [0:256:1]} | slice | bytes 262144 | tf_op jit(solution)/shard_map/slice | solution.py:27
  53.7 9.7 %slice.133 = bf16[4,8,8,256]{3,2,1,0:T(8,128)(2,1)} slice(bf16[10,17,17,256]{3,2,1,0:T(8,128)(2,1)S(1)} %fusion.38), slice={[0:8:2], [1:17:2], [0:16:2], [0:256:1]} | slice | bytes 262144 | tf_op jit(solution)/shard_map/slice | solution.py:27
  63.5 9.7 %slice.134 = bf16[4,8,8,256]{3,2,1,0:T(8,128)(2,1)} slice(bf16[10,17,17,256]{3,2,1,0:T(8,128)(2,1)S(1)} %fusion.38), slice={[0:8:2], [1:17:2], [1:17:2], [0:256:1]} | slice | bytes 262144 | tf_op jit(solution)/shard_map/slice | solution.py:27
  73.2 9.8 %slice.135 = bf16[4,8,8,256]{3,2,1,0:T(8,128)(2,1)} slice(bf16[10,17,17,256]{3,2,1,0:T(8,128)(2,1)S(1)} %fusion.38), slice={[0:8:2], [1:17:2], [2:17:2], [0:256:1]} | slice | bytes 262144 | tf_op jit(solution)/shard_map/slice | solution.py:27
  82.9 9.7 %slice.136 = bf16[4,8,8,256]{3,2,1,0:T(8,128)(2,1)} slice(bf16[10,17,17,256]{3,2,1,0:T(8,128)(2,1)S(1)} %fusion.38), slice={[0:8:2], [2:17:2], [0:16:2], [0:256:1]} | slice | bytes 262144 | tf_op jit(solution)/shard_map/slice | solution.py:27
  92.6 9.7 %slice.137 = bf16[4,8,8,256]{3,2,1,0:T(8,128)(2,1)} slice(bf16[10,17,17,256]{3,2,1,0:T(8,128)(2,1)S(1)} %fusion.38), slice={[0:8:2], [2:17:2], [1:17:2], [0:256:1]} | slice | bytes 262144 | tf_op jit(solution)/shard_map/slice | solution.py:27
  102.4 9.7 %slice.138 = bf16[4,8,8,256]{3,2,1,0:T(8,128)(2,1)} slice(bf16[10,17,17,256]{3,2,1,0:T(8,128)(2,1)S(1)} %fusion.38), slice={[0:8:2], [2:17:2], [2:17:2], [0:256:1]} | slice | bytes 262144 | tf_op jit(solution)/shard_map/slice | solution.py:27
  112.1 9.7 %slice.139 = bf16[4,8,8,256]{3,2,1,0:T(8,128)(2,1)} slice(bf16[10,17,17,256]{3,2,1,0:T(8,128)(2,1)S(1)} %fusion.38), slice={[1:9:2], [0:16:2], [0:16:2], [0:256:1]} | slice | bytes 262144 | tf_op jit(solution)/shard_map/slice | solution.py:27
  121.8 9.7 %slice.140 = bf16[4,8,8,256]{3,2,1,0:T(8,128)(2,1)} slice(bf16[10,17,17,256]{3,2,1,0:T(8,128)(2,1)S(1)} %fusion.38), slice={[1:9:2], [0:16:2], [1:17:2], [0:256:1]} | slice | bytes 262144 | tf_op jit(solution)/shard_map/slice | solution.py:27
  131.5 9.7 %slice.141 = bf16[4,8,8,256]{3,2,1,0:T(8,128)(2,1)} slice(bf16[10,17,17,256]{3,2,1,0:T(8,128)(2,1)S(1)} %fusion.38), slice={[1:9:2], [0:16:2], [2:17:2], [0:256:1]} | slice | bytes 262144 | tf_op jit(solution)/shard_map/slice | solution.py:27
  141.3 9.7 %slice.142 = bf16[4,8,8,256]{3,2,1,0:T(8,128)(2,1)} slice(bf16[10,17,17,256]{3,2,1,0:T(8,128)(2,1)S(1)} %fusion.38), slice={[1:9:2], [1:17:2], [0:16:2], [0:256:1]} | slice | bytes 262144 | tf_op jit(solution)/shard_map/slice | solution.py:27
  151.0 9.7 %slice.143 = bf16[4,8,8,256]{3,2,1,0:T(8,128)(2,1)} slice(bf16[10,17,17,256]{3,2,1,0:T(8,128)(2,1)S(1)} %fusion.38), slice={[1:9:2], [1:17:2], [1:17:2], [0:256:1]} | slice | bytes 262144 | tf_op jit(solution)/shard_map/slice | solution.py:27
  160.7 9.8 %slice.144 = bf16[4,8,8,256]{3,2,1,0:T(8,128)(2,1)} slice(bf16[10,17,17,256]{3,2,1,0:T(8,128)(2,1)S(1)} %fusion.38), slice={[1:9:2], [1:17:2], [2:17:2], [0:256:1]} | slice | bytes 262144 | tf_op jit(solution)/shard_map/slice | solution.py:27
  170.5 9.7 %slice.145 = bf16[4,8,8,256]{3,2,1,0:T(8,128)(2,1)} slice(bf16[10,17,17,256]{3,2,1,0:T(8,128)(2,1)S(1)} %fusion.38), slice={[1:9:2], [2:17:2], [0:16:2], [0:256:1]} | slice | bytes 262144 | tf_op jit(solution)/shard_map/slice | solution.py:27
  180.2 9.7 %slice.146 = bf16[4,8,8,256]{3,2,1,0:T(8,128)(2,1)} slice(bf16[10,17,17,256]{3,2,1,0:T(8,128)(2,1)S(1)} %fusion.38), slice={[1:9:2], [2:17:2], [1:17:2], [0:256:1]} | slice | bytes 262144 | tf_op jit(solution)/shard_map/slice | solution.py:27
  189.9 1.5 slice.147
  196.3 1.2 slice.154
  197.5 1.2 slice.155
  198.7 1.5 slice.156
  200.3 1.0 constant_dynamic-update-slice_fusion.26
  201.2 0.9 constant_dynamic-update-slice_fusion.25
  202.2 0.9 constant_dynamic-update-slice_fusion.24
  203.1 0.9 constant_dynamic-update-slice_fusion.23
  213.5 1.8 copy-done.3
  215.3 4.0 fusion.43
  220.3 176.8 %all-gather.6.cloned.1.call-done = f32[27648,256]{1,0:T(8,128)} async-done(((f32[6912,256]{1,0:T(8,128)}), f32[27648,256]{1,0:T(8,128)}) %all-gather.6.cloned.1.call-update) | async-done | bytes 28311568 | tf_op jit(solution)/shard_map/all_gather | solution.py:11
  397.1 15.0 %reduce_sum.85 = f32[6912,256]{1,0:T(8,128)} reduce(f32[4,6912,256]{2,1,0:T(8,128)} %bitcast.129, f32[]{:T(128)} %constant.4.clone.1), dimensions={0}, to_apply=%region_12.13 | reduce | flops 5308416 | bytes 35389444 | tf_op jit(solution)/shard_map/reduce_sum | solution.py:12
  412.4 52.1 %all-gather.4.cloned.1.call-done = bf16[6912,256]{1,0:T(8,128)(2,1)} async-done(((bf16[864,256]{1,0:T(8,128)(2,1)}), bf16[6912,256]{1,0:T(8,128)(2,1)}) %all-gather.4.cloned.1.call-update) | async-done | bytes 3538960 | tf_op jit(solution)/shard_map/all_gather | solution.py:101
  464.5 3.1 convolution_bitcast_fusion
  474.3 3.1 copy.39
  477.4 3.5 reshape.271
  480.9 1.4 slice.183
  482.3 1.5 collective-permute-start.1
  483.8 1.9 slice_bitcast_fusion.7
  485.8 3.9 convolution_convert_fusion
  489.6 1.3 fusion.39
  490.9 1.3 fusion.41
  492.7 9.5 %all-reduce.10 = (f32[32]{0:T(128)S(1)}, f32[32]{0:T(128)S(1)}) all-reduce(f32[32]{0:T(128)S(1)} %reduce_sum.84, f32[32]{0:T(128)S(1)} %reduce_sum.81), channel_id=1, replica_groups=mesh['dp'=8,'tm'=4] {'tm'}, use_global_device_ids=true, to_apply=%region_11.12 | all-reduce | flops 64 | bytes 512 | tf_op jit(solution)/shard_map/psum | solution.py:113
  502.5 1.6 fusion.37
  504.1 92.2 %reduce-scatter.2.cloned.1.call-done = f32[864,256]{1,0:T(8,128)} async-done(((f32[6912,256]{1,0:T(8,128)}), f32[864,256]{1,0:T(8,128)}) %reduce-scatter.2.cloned.1.call-update) | async-done | bytes 884752 | tf_op jit(solution)/shard_map/reduce_scatter | solution.py:129
  (92 shorter events, 23.7 us)
Async XLA Ops:
  7.2 206.3 %copy-start = (bf16[1,4,8,8,256]{4,3,2,1,0:T(8,128)(2,1)S(1)}, bf16[1,4,8,8,256]{4,3,2,1,0:T(8,128)(2,1)}, u32[]{:S(2)}) copy-start(bf16[1,4,8,8,256]{4,3,2,1,0:T(8,128)(2,1)} %param.11) | copy-start | bytes 393220
  7.2 389.9 %all-gather.6.cloned.1.call-start = ((), (), s32[]{:S(2)}) async-start(), calls=%async_computation.3 | async-start | bytes 35389440 | tf_op jit(solution)/shard_map/all_gather | solution.py:11
  21.0 2.4 collective-permute-start
  200.3 12.9 %copy-start.7 = (bf16[4,8,8,256]{3,2,1,0:T(8,128)(2,1)S(1)}, bf16[4,8,8,256]{3,2,1,0:T(8,128)(2,1)}, u32[]{:S(2)}) copy-start(bf16[4,8,8,256]{3,2,1,0:T(8,128)(2,1)} %slice.144) | copy-start | bytes 393220
  200.3 13.0 %copy-start.6 = (bf16[4,8,8,256]{3,2,1,0:T(8,128)(2,1)S(1)}, bf16[4,8,8,256]{3,2,1,0:T(8,128)(2,1)}, u32[]{:S(2)}) copy-start(bf16[4,8,8,256]{3,2,1,0:T(8,128)(2,1)} %slice.145) | copy-start | bytes 393220
  200.3 13.0 %copy-start.5 = (bf16[4,8,8,256]{3,2,1,0:T(8,128)(2,1)S(1)}, bf16[4,8,8,256]{3,2,1,0:T(8,128)(2,1)}, u32[]{:S(2)}) copy-start(bf16[4,8,8,256]{3,2,1,0:T(8,128)(2,1)} %slice.146) | copy-start | bytes 393220
  213.5 1.8 copy-start.3
  219.3 245.2 %all-gather.4.cloned.1.call-start = ((), (), s32[]{:S(2)}) async-start(), calls=%async_computation.1 | async-start | bytes 3981312 | tf_op jit(solution)/shard_map/all_gather | solution.py:101
  220.0 376.2 %reduce-scatter.2.cloned.1.call-start = ((), (), s32[]{:S(2)}) async-start(), calls=%async_computation.2 | async-start | bytes 7962624 | tf_op jit(solution)/shard_map/reduce_scatter | solution.py:129
  480.9 4.8 copy-start.4
  482.3 7.3 %collective-permute-start.1 = (f32[2,16,16,256]{3,2,1,0:T(8,128)S(1)}, f32[2,16,16,256]{3,2,1,0:T(8,128)S(1)}, u32[]{:S(2)}, u32[]{:S(2)}) collective-permute-start(f32[2,16,16,256]{3,2,1,0:T(8,128)S(1)} %slice.183), channel_id=1, source_target_pairs={{1,0},{2,1},{3,2},{5,4},{6,5},{7,6},{9,8},{10,9},{11,10},{13,12},{... | collective-permute-start | bytes 1572872 | tf_op jit(solution)/shard_map/ppermute | solution.py:19
  485.7 5.2 copy-start.2
  485.7 5.2 copy-start.8
  485.8 5.2 copy-start.9
  489.6 106.6 %copy-start.1 = (bf16[1,4,8,8,256]{4,3,2,1,0:T(8,128)(2,1)S(1)}, bf16[1,4,8,8,256]{4,3,2,1,0:T(8,128)(2,1)}, u32[]{:S(2)}) copy-start(bf16[1,4,8,8,256]{4,3,2,1,0:T(8,128)(2,1)} %param.11) | copy-start | bytes 393220
Sparse Core Ops, SparseCore 0:
  219.4 177.6 all-gather.5
  399.3 65.1 all-gather.3
  468.8 127.4 reduce-scatter.1
